TPU v7x, 32 devices: a whole 2x2x4 slice. The times are simulated.
32 devices in a mesh: seq: 8 (over z, x), head: 4 (over y, core).
Axes of the slice: x: 2, y: 2, z: 4, core: 2. Of those that a mesh axis runs over, the one named last changes fastest.
Arguments:
- query_rows: bfloat16 [16384, 1024], P('seq', 'head'), may hold values from -8 to 8
- key_rows: bfloat16 [16384, 1024], P('seq', 'head'), may hold values from -6 to 6
- value_rows: bfloat16 [16384, 1024], P('seq', 'head'), may hold values from -12 to 12
- out_grad: bfloat16 [16384, 1024], P('seq', 'head'), may hold values from -12 to 12
- block_perm: int32 [8, 64], P('head'), may hold values from 0 to 63, as said below
- cut_count: int32 [8], P('head'), may hold values from 1 to 4, as said below
- norm_gain: float32 [1024], P('head'), may hold values from 0.1 to 1.9
Outputs:
- normed_out: bfloat16 [16384, 1024], P('seq', 'head')
- query_grad: bfloat16 [16384, 1024], P('seq', 'head')
- key_grad: bfloat16 [16384, 1024], P('seq', 'head')
- value_grad: bfloat16 [16384, 1024], P('seq', 'head')
- gain_grad: float32 [1024], P('head')
Inputs may be any that keep to these rules, and one draw needn't show every extreme that they name: `block_perm`: each row is a permutation of 0 to 63. For every head, of the 8 blocks d * 8 to (d + 1) * 8 - 1, at most 1 are paired with blocks of one range s * 8 to (s + 1) * 8 - 1, and some pair (d, s) reaches 1. `cut_count`: some head has exactly 4.
All inputs are finite; a program needn't handle non-finite values.
Results may differ from a plain program's by a relative error of at most 0.0071.
Values may be sent and summed in bfloat16 or wider, within the bound.
A program may use at most 128 MiB of HBM per device.

v0:
```python
from functools import partial
import jax
import jax.numpy as jnp
from jax import lax
from jax.sharding import PartitionSpec as P

BLOCK = 256
KCUT = 4


def split_heads(rows, heads):
    tokens = rows.shape[0]
    width = rows.shape[1] // heads
    return rows.reshape(tokens // BLOCK, BLOCK, heads, width).transpose(2, 0, 1, 3)


def merge_heads(parts):
    return parts.transpose(1, 2, 0, 3).reshape(
        parts.shape[1] * parts.shape[2], parts.shape[0] * parts.shape[3]
    )


def to_slots(rows, slot_of, count):
    match = slot_of[:, None, :] == jnp.arange(count)[None, :, None]
    chosen = jnp.sum(jnp.where(match, jnp.arange(rows.shape[1])[None, None, :], 0), axis=2)
    filled = jnp.any(match, axis=2)
    picked = jax.vmap(lambda piece, which: piece[which])(rows, chosen)
    shape = filled.shape + (1,) * (rows.ndim - 2)
    return jnp.where(filled.reshape(shape), picked, jnp.zeros_like(picked))


def from_slots(slot_rows, slot_of):
    return jax.vmap(lambda piece, which: piece[which])(slot_rows, slot_of)


def attend(query, own_rows, paired_rows, cutoff_rows, live, scale):
    width = query.shape[-1]
    span = own_rows.shape[1]
    count = cutoff_rows.shape[0]
    own = jnp.einsum(
        "gqd,gkd->gqk", query, own_rows[..., :width], preferred_element_type=jnp.float32
    )
    pair = jnp.einsum(
        "gqd,gkd->gqk", query, paired_rows[..., :width], preferred_element_type=jnp.float32
    )
    cut = jnp.einsum(
        "gqd,ckd->gqck", query, cutoff_rows[..., :width], preferred_element_type=jnp.float32
    )
    cut = cut.reshape(query.shape[0], query.shape[1], count * span)
    scores = jnp.concatenate([own, pair, cut], axis=-1) * scale
    open_keys = jnp.concatenate([jnp.ones((2 * span,), jnp.bool_), jnp.repeat(live, span)])
    scores = jnp.where(open_keys, scores, -1e30)
    top = jnp.max(scores, axis=-1)
    weights = jnp.exp(scores - top[..., None])
    total = jnp.sum(weights, axis=-1)
    return (weights / total[..., None], top, total)


def forward_head(query, own_rows, paired_rows, cutoff_rows, live, scale):
    width = query.shape[-1]
    span = query.shape[1]
    groups = query.shape[0] // 2
    count = cutoff_rows.shape[0]

    def forward_step(pieces):
        query_part, own_part, pair_part = pieces
        prob, top, total = attend(query_part, own_part, pair_part, cutoff_rows, live, scale)
        weights = prob.astype(jnp.bfloat16)
        result = jnp.einsum(
            "gqk,gkd->gqd",
            weights[..., :span],
            own_part[..., width:],
            preferred_element_type=jnp.float32,
        )
        result = result + jnp.einsum(
            "gqk,gkd->gqd",
            weights[..., span : 2 * span],
            pair_part[..., width:],
            preferred_element_type=jnp.float32,
        )
        cut_weight = weights[..., 2 * span :].reshape(2, span, count, span)
        result = result + jnp.einsum(
            "gqck,ckd->gqd",
            cut_weight,
            cutoff_rows[..., width:],
            preferred_element_type=jnp.float32,
        )
        return result.astype(jnp.bfloat16)

    result = lax.map(
        forward_step,
        (
            query.reshape(groups, 2, span, width),
            own_rows.reshape(groups, 2, span, 2 * width),
            paired_rows.reshape(groups, 2, span, 2 * width),
        ),
    )
    return result.reshape(query.shape)


def backward_head(query, own_rows, paired_rows, cutoff_rows, live, cotangent, scale):
    width = query.shape[-1]
    span = query.shape[1]
    groups = query.shape[0] // 2
    count = cutoff_rows.shape[0]

    def backward_step(carry, pieces):
        query_part, own_part, pair_part, cot_part = pieces
        prob, top, total = attend(query_part, own_part, pair_part, cutoff_rows, live, scale)
        weights = prob.astype(jnp.bfloat16)
        dprob = jnp.concatenate(
            [
                jnp.einsum(
                    "gqd,gkd->gqk",
                    cot_part,
                    own_part[..., width:],
                    preferred_element_type=jnp.float32,
                ),
                jnp.einsum(
                    "gqd,gkd->gqk",
                    cot_part,
                    pair_part[..., width:],
                    preferred_element_type=jnp.float32,
                ),
                jnp.einsum(
                    "gqd,ckd->gqck",
                    cot_part,
                    cutoff_rows[..., width:],
                    preferred_element_type=jnp.float32,
                ).reshape(2, span, count * span),
            ],
            axis=-1,
        )
        delta = jnp.sum(prob * dprob, axis=-1)
        dscore = (prob * (dprob - delta[..., None]) * scale).astype(jnp.bfloat16)
        cut_score = dscore[..., 2 * span :].reshape(2, span, count, span)
        cut_weight = weights[..., 2 * span :].reshape(2, span, count, span)
        query_grad = jnp.einsum(
            "gqk,gkd->gqd",
            dscore[..., :span],
            own_part[..., :width],
            preferred_element_type=jnp.float32,
        )
        query_grad = query_grad + jnp.einsum(
            "gqk,gkd->gqd",
            dscore[..., span : 2 * span],
            pair_part[..., :width],
            preferred_element_type=jnp.float32,
        )
        query_grad = query_grad + jnp.einsum(
            "gqck,ckd->gqd", cut_score, cutoff_rows[..., :width], preferred_element_type=jnp.float32
        )
        own_grad = jnp.concatenate(
            [
                jnp.einsum(
                    "gqk,gqd->gkd",
                    dscore[..., :span],
                    query_part,
                    preferred_element_type=jnp.float32,
                ),
                jnp.einsum(
                    "gqk,gqd->gkd",
                    weights[..., :span],
                    cot_part,
                    preferred_element_type=jnp.float32,
                ),
            ],
            axis=-1,
        )
        pair_grad = jnp.concatenate(
            [
                jnp.einsum(
                    "gqk,gqd->gkd",
                    dscore[..., span : 2 * span],
                    query_part,
                    preferred_element_type=jnp.float32,
                ),
                jnp.einsum(
                    "gqk,gqd->gkd",
                    weights[..., span : 2 * span],
                    cot_part,
                    preferred_element_type=jnp.float32,
                ),
            ],
            axis=-1,
        )
        cut_grad = jnp.concatenate(
            [
                jnp.einsum(
                    "gqck,gqd->ckd", cut_score, query_part, preferred_element_type=jnp.float32
                ),
                jnp.einsum(
                    "gqck,gqd->ckd", cut_weight, cot_part, preferred_element_type=jnp.float32
                ),
            ],
            axis=-1,
        )
        return (
            carry + cut_grad,
            (query_grad.astype(jnp.bfloat16), own_grad, pair_grad, top, total, delta),
        )

    start = jnp.zeros((count, span, 2 * width), jnp.float32)
    cut_sum, outputs = lax.scan(
        backward_step,
        start,
        (
            query.reshape(groups, 2, span, width),
            own_rows.reshape(groups, 2, span, 2 * width),
            paired_rows.reshape(groups, 2, span, 2 * width),
            cotangent.reshape(groups, 2, span, width),
        ),
    )
    query_grad, own_grad, pair_grad, top, total, delta = outputs
    blocks = query.shape[0]
    return (
        query_grad.reshape(query.shape),
        own_grad.reshape(own_rows.shape),
        pair_grad.reshape(own_rows.shape),
        cut_sum,
        top.reshape(blocks, span),
        total.reshape(blocks, span),
        delta.reshape(blocks, span),
    )


def owner_pair(query, cotangent, top, total, delta, own_rows, scale):
    width = query.shape[-1]
    scores = (
        jnp.einsum("jqd,jkd->jqk", query, own_rows[..., :width], preferred_element_type=jnp.float32)
        * scale
    )
    prob = jnp.exp(scores - top[..., None]) / total[..., None]
    dprob = jnp.einsum(
        "jqd,jkd->jqk", cotangent, own_rows[..., width:], preferred_element_type=jnp.float32
    )
    dscore = (prob * (dprob - delta[..., None]) * scale).astype(jnp.bfloat16)
    return jnp.concatenate(
        [
            jnp.einsum("jqk,jqd->jkd", dscore, query, preferred_element_type=jnp.float32),
            jnp.einsum(
                "jqk,jqd->jkd",
                prob.astype(jnp.bfloat16),
                cotangent,
                preferred_element_type=jnp.float32,
            ),
        ],
        axis=-1,
    )


def body(query_rows, key_rows, value_rows, out_grad, block_perm, cut_count, norm_gain):
    heads = block_perm.shape[0]
    width = query_rows.shape[1] // heads
    blocks = query_rows.shape[0] // BLOCK
    seq_count = lax.axis_size("seq")
    head_count = lax.axis_size("head")
    capacity = (blocks + seq_count - 1) // seq_count
    slot_count = seq_count * capacity
    scale = width ** (-0.5)
    position = lax.axis_index("seq")
    query_h = split_heads(query_rows, heads)
    grad_h = split_heads(out_grad, heads)
    own_rows = jnp.concatenate(
        [split_heads(key_rows, heads), split_heads(value_rows, heads)], axis=-1
    )
    local_perm = lax.dynamic_slice_in_dim(block_perm, position * blocks, blocks, 1)
    source_dev = local_perm // blocks
    lower = jnp.arange(blocks)[:, None] > jnp.arange(blocks)[None, :]
    same_source = source_dev[:, :, None] == source_dev[:, None, :]
    recv_slot = source_dev * capacity + jnp.sum(same_source & lower[None], axis=2)
    owned = position * blocks + jnp.arange(blocks)
    hits = block_perm[:, None, :] == owned[None, :, None]
    dest_global = jnp.sum(
        jnp.where(hits, jnp.arange(block_perm.shape[1])[None, None, :], 0), axis=2
    )
    dest_dev = dest_global // blocks
    dest_local = dest_global % blocks
    before = (dest_dev[:, :, None] == dest_dev[:, None, :]) & (
        dest_local[:, None, :] < dest_local[:, :, None]
    )
    send_slot = dest_dev * capacity + jnp.sum(before, axis=2)
    own_send = to_slots(own_rows, send_slot, slot_count)
    query_send = to_slots(query_h, recv_slot, slot_count)
    own_recv, query_recv = (
        lax.all_to_all(own_send, "seq", split_axis=1, concat_axis=1, tiled=True),
        lax.all_to_all(query_send, "seq", split_axis=1, concat_axis=1, tiled=True),
    )
    query_owner = from_slots(query_recv, send_slot)
    paired_rows = from_slots(own_recv, recv_slot)
    cut_global = block_perm[:, :KCUT]
    cut_dev = cut_global // blocks
    cut_local = cut_global % blocks
    cut_pick = jax.vmap(lambda piece, which: piece[which])(own_rows, cut_local)
    cut_pick = jnp.where(
        (cut_dev == position)[:, :, None, None], cut_pick, jnp.zeros_like(cut_pick)
    )
    cutoff_rows = lax.psum(cut_pick.astype(jnp.float32).astype(jnp.bfloat16), "seq")
    live = jnp.arange(KCUT)[None, :] < cut_count[:, None]
    attn = jax.vmap(partial(forward_head, scale=scale))(
        query_h, own_rows, paired_rows, cutoff_rows, live
    )
    attn_f = attn.astype(jnp.float32)
    grad_f = grad_h.astype(jnp.float32)
    gain = norm_gain.reshape(heads, 1, 1, width)
    square_part = jnp.sum(attn_f * attn_f, axis=(0, 3))
    mix_part = jnp.sum(gain * grad_f * attn_f, axis=(0, 3))
    square_sum, mix_sum = lax.psum((square_part, mix_part), "head")
    features = head_count * heads * width
    scale_row = lax.rsqrt(square_sum / features + 1e-06)[None, :, :, None]
    normed = (attn_f * scale_row * gain).astype(jnp.bfloat16)
    gain_part = jnp.sum(grad_f * attn_f * scale_row, axis=(1, 2))
    cotangent = (
        scale_row * gain * grad_f - attn_f * scale_row**3 * mix_sum[None, :, :, None] / features
    ).astype(jnp.bfloat16)
    query_grad, own_grad, pair_grad, cut_grad, top, total, delta = jax.vmap(
        partial(backward_head, scale=scale)
    )(query_h, own_rows, paired_rows, cutoff_rows, live, cotangent)
    cot_send = to_slots(cotangent, recv_slot, slot_count)
    cot_recv = lax.all_to_all(cot_send, "seq", split_axis=1, concat_axis=1, tiled=True)
    top_send = to_slots(top, recv_slot, slot_count)
    total_send = to_slots(total, recv_slot, slot_count)
    delta_send = to_slots(delta, recv_slot, slot_count)
    top_recv, total_recv, delta_recv = (
        lax.all_to_all(top_send, "seq", split_axis=1, concat_axis=1, tiled=True),
        lax.all_to_all(total_send, "seq", split_axis=1, concat_axis=1, tiled=True),
        lax.all_to_all(delta_send, "seq", split_axis=1, concat_axis=1, tiled=True),
    )
    pair_full = jax.vmap(partial(owner_pair, scale=scale))(
        query_owner,
        from_slots(cot_recv, send_slot),
        from_slots(top_recv, send_slot),
        from_slots(total_recv, send_slot),
        from_slots(delta_recv, send_slot),
        own_rows,
    )
    pair_term = lax.optimization_barrier(pair_full.astype(jnp.bfloat16)).astype(jnp.float32)
    cut_total, gain_total = lax.psum((cut_grad, gain_part), "seq")
    match = (
        (cut_dev == position)[:, :, None]
        & (cut_local[:, :, None] == jnp.arange(blocks)[None, None, :])
    ).astype(jnp.float32)
    cut_term = jnp.einsum("hcj,hcqd->hjqd", match, cut_total, precision=lax.Precision.HIGHEST)
    total_grad = (own_grad + pair_term + cut_term).astype(jnp.bfloat16)
    return (
        merge_heads(normed),
        merge_heads(query_grad),
        merge_heads(total_grad[..., :width]),
        merge_heads(total_grad[..., width:]),
        gain_total.reshape(heads * width),
    )


def solution(mesh):
    placed = (
        P("seq", "head"),
        P("seq", "head"),
        P("seq", "head"),
        P("seq", "head"),
        P("head", None),
        P("head"),
        P("head"),
    )
    return jax.shard_map(
        body,
        mesh=mesh,
        in_specs=placed,
        out_specs=(
            P("seq", "head"),
            P("seq", "head"),
            P("seq", "head"),
            P("seq", "head"),
            P("head"),
        ),
        check_vma=False,
    )
```

profile of v0, /device:TPU:0, one launch (start us, length us, event | category | flops | bytes accessed | tf_op | source)
XLA Modules:
  0.0 683.0 jit_solution(10543006544791201384)
XLA Ops:
  19.0 7.3 %all-to-all-start = ((bf16[2,8,256,256]{3,2,0,1:T(8,128)(2,1)}), bf16[2,8,256,256]{3,2,0,1:T(8,128)(2,1)}, u32[]{:S(2)}, u32[]{:S(2)}) async-start(bf16[2,8,256,256]{3,2,0,1:T(8,128)(2,1)} %copy_select_fusion), calls=%async_computation | async-start | bytes 4194304 | tf_op jit(solution)/shard_map/all_to_all | solution.py:286
  36.0 51.3 %all-to-all-done = bf16[2,8,256,256]{3,2,0,1:T(8,128)(2,1)} async-done(((bf16[2,8,256,256]{3,2,0,1:T(8,128)(2,1)}), bf16[2,8,256,256]{3,2,0,1:T(8,128)(2,1)}, u32[]{:S(2)}, u32[]{:S(2)}) %all-to-all-start) | async-done | bytes 2097184 | tf_op jit(solution)/shard_map/all_to_all | solution.py:286
  94.2 40.7 %all-reduce.5.cloned.1.call-done = bf16[2,4,256,256]{3,2,1,0:T(8,128)(2,1)} async-done(((bf16[2,4,256,256]{3,2,1,0:T(8,128)(2,1)}), bf16[2,4,256,256]{3,2,1,0:T(8,128)(2,1)}) %all-reduce.5.cloned.1.call-update) | async-done | bytes 1048592 | tf_op jit(solution)/shard_map/psum | solution.py:298
  136.1 76.6 %while.32 = (s32[]{:T(128)}, bf16[4,2,2,256,128]{4,3,2,0,1:T(8,128)(2,1)}, bf16[4,2,2,256,128]{4,3,2,1,0:T(8,128)(2,1)S(1)}, bf16[4,2,2,256,256]{4,3,2,1,0:T(8,1...) while((s32[]{:T(128)}, ...), condition=%wide.region_9.10_spmd.clone, body=%wide.region_6.9_spmd.clone.sunk | while | flops 818284032 | bytes 55597728 | solution.py:90
  142.7 5.4 copy.414
  161.8 5.4 copy.414
  181.0 5.4 copy.414
  200.1 5.4 copy.414
  217.2 6.9 %psum.36 = f32[8,256]{1,0:T(8,128)S(1)} all-reduce(f32[8,256]{1,0:T(8,128)S(1)} %reduce_sum.131), channel_id=1, replica_groups=mesh['seq'=8,'head'=4] {'head'}, use_global_device_ids=true, to_apply=%region_11.12 | all-reduce | flops 2048 | bytes 16384 | tf_op jit(solution)/shard_map/psum | solution.py:308
  227.0 6.3 psum.37
  237.7 237.2 %while.33 = (s32[]{:T(128)}, f32[2,4,256,256]{2,3,1,0:T(8,128)}, bf16[4,2,2,256,128]{4,3,2,0,1:T(8,128)(2,1)}, f32[4,2,2,256,256]{3,4,2,1,0:T(8,128)}, f32[4,2,2...) while((s32[]{:T(128)}, f32[2,4,256,256]{2,3,1,0:T(8,128)}, ...), condition=%wide.region_18.19_spmd.clone, body=%wide.region_14.18_spmd.clone.sunk | while | flops 1934750720 | bytes 244144336 | solution.py:204
  243.4 5.4 copy.417
  258.1 5.4 copy.416
  263.5 5.6 multiply_reduce_fusion.3
  302.2 5.4 copy.417
  316.8 5.4 copy.416
  322.2 5.6 multiply_reduce_fusion.3
  361.7 5.4 copy.417
  376.3 5.4 copy.416
  381.7 5.6 multiply_reduce_fusion.3
  421.1 5.4 copy.417
  435.8 5.4 copy.416
  441.2 5.6 multiply_reduce_fusion.3
  477.6 9.9 %all_to_all.30 = f32[2,8,256]{2,0,1:T(2,128)S(1)} all-to-all(f32[2,8,256]{2,0,1:T(2,128)S(1)} %get-tuple-element.372), channel_id=1, replica_groups=mesh['seq'=8,'head'=4] {'seq'}, dimensions={1} | all-to-all | bytes 32768 | tf_op jit(solution)/shard_map/all_to_all | solution.py:325
  508.2 26.6 %all_to_all.31 = bf16[2,8,256,128]{3,2,0,1:T(8,128)(2,1)} all-to-all(bf16[2,8,256,128]{3,2,0,1:T(8,128)(2,1)} %get-tuple-element.373), channel_id=1, replica_groups=mesh['seq'=8,'head'=4] {'seq'}, dimensions={1} | all-to-all | bytes 2097152 | tf_op jit(solution)/shard_map/all_to_all | solution.py:287
  540.5 4.6 copy.287
  549.6 28.1 %psum.39 = f32[256]{0:T(256)} all-reduce(f32[256]{0:T(256)S(1)} %bitcast.413), channel_id=1, replica_groups=mesh['seq'=8,'head'=4] {'seq'}, use_global_device_ids=true, to_apply=%region_23.24 | all-reduce | flops 256 | bytes 2048 | tf_op jit(solution)/shard_map/psum | solution.py:338
  587.4 4.8 fusion.121
  593.5 63.7 %all-reduce.7.cloned.1.call-done = f32[2,4,256,256]{3,1,2,0:T(4,128)} async-done(((f32[2,4,256,256]{3,1,2,0:T(4,128)}), f32[2,4,256,256]{3,1,2,0:T(4,128)}) %all-reduce.7.cloned.1.call-update) | async-done | bytes 2097168 | tf_op jit(solution)/shard_map/psum | solution.py:338
  657.2 5.3 fusion.130
  662.5 5.3 copy.306
  667.8 4.4 add_convert_fusion
  (470 shorter events, 314.9 us)
Async XLA Ops:
  15.9 10.5 %copy-start.31 = (s32[2,64]{1,0:T(2,128)S(1)}, s32[2,64]{1,0:T(2,128)}, u32[]{:S(2)}) copy-start(s32[2,64]{1,0:T(2,128)} %param.15) | copy-start | bytes 1540
  19.0 68.4 %all-to-all-start = ((bf16[2,8,256,256]{3,2,0,1:T(8,128)(2,1)}), bf16[2,8,256,256]{3,2,0,1:T(8,128)(2,1)}, u32[]{:S(2)}, u32[]{:S(2)}) async-start(bf16[2,8,256,256]{3,2,0,1:T(8,128)(2,1)} %copy_select_fusion), calls=%async_computation | async-start | bytes 4194304 | tf_op jit(solution)/shard_map/all_to_all | solution.py:286
  26.3 108.6 %all-reduce.5.cloned.1.call-start = ((), (), s32[]{:S(2)}) async-start(), calls=%async_computation.6 | async-start | bytes 2097152 | tf_op jit(solution)/shard_map/psum | solution.py:298
  89.1 47.0 %copy-start.42 = (s32[2]{0:T(128)S(1)}, s32[2]{0:T(128)}, u32[]{:S(2)}) copy-start(s32[2]{0:T(128)} %param.16) | copy-start | bytes 28
  212.7 11.5 %copy-start.19 = (f32[8,256,2,128]{3,2,1,0:T(2,128)S(1)}, f32[8,256,2,128]{3,2,1,0:T(2,128)}, u32[]{:S(2)}) copy-start(f32[8,256,2,128]{3,2,1,0:T(2,128)} %reshape.418) | copy-start | bytes 6291460
  212.7 11.5 %copy-start.41 = (f32[256]{0:T(256)S(1)}, f32[256]{0:T(256)}, u32[]{:S(2)}) copy-start(f32[256]{0:T(256)} %param.17) | copy-start | bytes 3076
  237.7 237.3 %copy-start.28 = (s32[16]{0:T(128)S(1)}, s32[16]{0:T(128)}, u32[]{:S(2)}) copy-start(s32[16]{0:T(128)} %reshape.321) | copy-start | bytes 196
  237.7 239.1 %copy-start.39 = (pred[2,8]{0,1:T(8,128)(4,1)S(1)}, pred[2,8]{0,1:T(8,128)(4,1)}, u32[]{:S(2)}) copy-start(pred[2,8]{0,1:T(8,128)(4,1)} %copy.288) | copy-start | bytes 52
  237.7 5.7 copy-start.7
  263.5 6.2 copy-start.2
  263.5 6.4 copy-start.6
  280.8 5.7 copy-start.8
  296.5 5.7 copy-start.7
  322.2 6.2 copy-start.2
  322.2 6.4 copy-start.6
  339.6 5.7 copy-start.8
  356.0 5.7 copy-start.7
  381.7 6.2 copy-start.2
  381.7 6.4 copy-start.6
  399.0 5.7 copy-start.8
  415.4 5.7 copy-start.7
  441.2 6.2 copy-start.2
  441.2 6.4 copy-start.6
  458.5 5.7 copy-start.8
  487.5 9.8 %all-to-all-start.3 = ((f32[2,8,256]{2,0,1:T(2,128)}), f32[2,8,256]{2,0,1:T(2,128)S(1)}, u32[]{:S(2)}, u32[]{:S(2)}) async-start(f32[2,8,256]{2,0,1:T(2,128)} %get-tuple-element.371), calls=%async_computation.3 | async-start | bytes 32768 | tf_op jit(solution)/shard_map/all_to_all | solution.py:326
  497.3 10.9 %all-to-all-start.5 = ((f32[2,8,256]{2,0,1:T(2,128)}), f32[2,8,256]{2,0,1:T(2,128)S(1)}, u32[]{:S(2)}, u32[]{:S(2)}) async-start(f32[2,8,256]{2,0,1:T(2,128)} %get-tuple-element.370), calls=%async_computation.5 | async-start | bytes 32768 | tf_op jit(solution)/shard_map/all_to_all | solution.py:327
  501.6 36.9 %copy-start.17 = (f32[2,4,256,256]{2,3,1,0:T(8,128)S(1)}, f32[2,4,256,256]{2,3,1,0:T(8,128)}, u32[]{:S(2)}) copy-start(f32[2,4,256,256]{2,3,1,0:T(8,128)} %get-tuple-element.120) | copy-start | bytes 6291460
  534.8 46.5 %all-to-all-start.4 = ((bf16[2,8,256,128]{3,2,0,1:T(8,128)(2,1)}), bf16[2,8,256,128]{3,2,0,1:T(8,128)(2,1)S(1)}, u32[]{:S(2)}, u32[]{:S(2)}) async-start(bf16[2,8,256,128]{3,2,0,1:T(8,128)(2,1)} %get-tuple-element.374), calls=%async_computation.4 | async-start | bytes 2097152 | tf_op jit(solution)/shard_map/all_to_all | solution.py:320
  538.5 118.7 %all-reduce.7.cloned.1.call-start = ((), (), s32[]{:S(2)}) async-start(), calls=%async_computation.7 | async-start | bytes 4194304 | tf_op jit(solution)/shard_map/psum | solution.py:338
  545.2 34.3 %copy-start.24 = (bf16[2,8,256,128]{3,2,0,1:T(8,128)(2,1)S(1)}, bf16[2,8,256,128]{3,2,0,1:T(8,128)(2,1)}, u32[]{:S(2)}) copy-start(bf16[2,8,256,128]{3,2,0,1:T(8,128)(2,1)} %all_to_all.31) | copy-start | bytes 3145732
  592.1 65.1 %copy-start.32 = (s32[2,4]{1,0:T(2,128)S(1)}, s32[2,4]{1,0:T(2,128)}, u32[]{:S(2)}) copy-start(s32[2,4]{1,0:T(2,128)} %get-tuple-element.351) | copy-start | bytes 100
  592.1 65.1 %copy-start.38 = (pred[2,4]{1,0:T(4,128)(4,1)S(1)}, pred[2,4]{1,0:T(4,128)(4,1)}, u32[]{:S(2)}) copy-start(pred[2,4]{1,0:T(4,128)(4,1)} %copy-done.37) | copy-start | bytes 28
  (71 other events, 208.9 us)
Sparse Core Ops, SparseCore 0:
  31.2 103.6 all-reduce.4
  542.9 114.2 all-reduce.6
where the time goes:
time: 686 us; the launch traced here: 683 us
  local copies, waits for them, and re-layouts  173 us (25%)
  waiting for transfers between devices  161 us (23%)
  matrix products  123 us (18%)
  other arithmetic  114 us (17%)
  blocking collectives  77.8 us (11%)
  starting transfers between devices  18.7 us (3%)
  between operations  14.6 us (2%)
    psum x1, waiting for transfers between devices, body(): cut_total, gain_total = lax.psum((cut_grad, gain_part), 'seq')  63.7 us
    all_to_all x1, waiting for transfers between devices, body(): lax.all_to_all(own_send, 'seq', split_axis=1, concat_axis=1, tiled=True)  51.3 us
    reshape x8, local copies, waits for them, and re-layouts, attend(): cut = cut.reshape(query.shape[0], query.shape[1], count * span)  43.2 us
    psum x1, waiting for transfers between devices, body(): lax.psum(cut_pick.astype(jnp.float32).astype(jnp.bfloat16), 'seq')  40.7 us
    psum x1, blocking collectives, body(): cut_total, gain_total = lax.psum((cut_grad, gain_part), 'seq')  28.1 us
    all_to_all x1, blocking collectives, body(): lax.all_to_all(query_send, 'seq', split_axis=1, concat_axis=1, tiled=True)  26.6 us
    reduce_sum x4, other arithmetic, backward_step(): delta = jnp.sum(prob * dprob, axis=-1)  22.4 us
    reshape x4, local copies, waits for them, and re-layouts, backward_step(): dprob = jnp.concatenate([jnp.einsum('gqd,gkd->gqk', cot_part, own_part[.....  21.7 us
  transfers between devices with their start and end apart: 6, of which 5 were waited for; matrix products, arithmetic and copies ran while one was open for 7% of the time, Pallas kernels for 0%

commit v1 on v0

--- a/solution.py
+++ b/solution.py
@@ -1,3 +1,4 @@
+import functools
 from functools import partial
 import jax
 import jax.numpy as jnp
@@ -6,6 +7,31 @@
 
 BLOCK = 256
 KCUT = 4
+
+
+def test_group(in_array, dim_at, axis_no):
+    field_out = jax.lax.axis_size("seq")
+    row_out, work_now = (field_out, jax.lax.axis_index("seq"))
+    frame_out = in_array.shape[dim_at] // row_out
+    state_now = jnp.roll(in_array, -work_now * frame_out, axis=dim_at)
+    in_order = [lax.slice_in_dim(state_now, 0, frame_out, axis=dim_at)]
+    for dev_j in range(1, row_out):
+        block_now = lax.slice_in_dim(
+            state_now, dev_j * frame_out, (dev_j + 1) * frame_out, axis=dim_at
+        )
+        in_order.append(
+            jax.lax.ppermute(
+                block_now,
+                axis_name="seq",
+                perm=[(i, (i + dev_j) % row_out) for i in range(row_out)],
+            )
+        )
+    answer = jnp.concatenate(in_order[::-1], axis=axis_no)
+    after = jnp.roll(answer, (work_now + 1) * in_order[0].shape[axis_no], axis=axis_no)
+    return after
+
+
+guide_the_meshes = functools.partial(test_group, dim_at=1, axis_no=1)
 
 
 def split_heads(rows, heads):
@@ -283,7 +309,7 @@
     own_send = to_slots(own_rows, send_slot, slot_count)
     query_send = to_slots(query_h, recv_slot, slot_count)
     own_recv, query_recv = (
-        lax.all_to_all(own_send, "seq", split_axis=1, concat_axis=1, tiled=True),
+        guide_the_meshes(own_send),
         lax.all_to_all(query_send, "seq", split_axis=1, concat_axis=1, tiled=True),
     )
     query_owner = from_slots(query_recv, send_slot)

time: 686 us -> 689 us (level)
    all_to_all x1 -> x0, waiting for transfers between devices: 51.3 us -> none  [body(): lax.all_to_all(own_send, 'seq', split_axis=1, concat_axis=1, tiled=True)]
    ppermute x0 -> x7, waiting for transfers between devices: none -> 37.8 us  [test_group(): jax.lax.ppermute(block_now, axis_name='seq', perm=[(i, (i + dev_j) % row_...]
    ppermute x0 -> x7, starting transfers between devices: none -> 12.5 us  [test_group(): jax.lax.ppermute(block_now, axis_name='seq', perm=[(i, (i + dev_j) % row_...]
    all_to_all x1 -> x0, starting transfers between devices: 7.28 us -> none  [body(): lax.all_to_all(own_send, 'seq', split_axis=1, concat_axis=1, tiled=True)]
    psum x1, waiting for transfers between devices: 40.7 us -> 47.7 us  [body(): lax.psum(cut_pick.astype(jnp.float32).astype(jnp.bfloat16), 'seq')]
    unnamed x61 -> x74, local copies, waits for them, and re-layouts: 17 us -> 22.6 us
  transfers between devices with their start and end apart: 6 -> 12, of which waited for: 5 -> 6; matrix products, arithmetic and copies ran while one was open for 7% -> 7% of each run, Pallas kernels for 0% -> 0%
where the time goes in v1:
time: 689 us; the launch traced here: 686 us
  local copies, waits for them, and re-layouts  177 us (26%)
  waiting for transfers between devices  158 us (23%)
  matrix products  124 us (18%)
  other arithmetic  111 us (16%)
  blocking collectives  76.9 us (11%)
  starting transfers between devices  22.7 us (3%)
  between operations  14.8 us (2%)
    psum x1, waiting for transfers between devices, body(): cut_total, gain_total = lax.psum((cut_grad, gain_part), 'seq')  64.2 us
    psum x1, waiting for transfers between devices, body(): lax.psum(cut_pick.astype(jnp.float32).astype(jnp.bfloat16), 'seq')  47.7 us
    reshape x8, local copies, waits for them, and re-layouts, attend(): cut = cut.reshape(query.shape[0], query.shape[1], count * span)  43.3 us
    ppermute x7, waiting for transfers between devices, test_group(): jax.lax.ppermute(block_now, axis_name='seq', perm=[(i, (i + dev_j) % row_...  37.8 us
    psum x1, blocking collectives, body(): cut_total, gain_total = lax.psum((cut_grad, gain_part), 'seq')  27.8 us
    all_to_all x1, blocking collectives, body(): lax.all_to_all(query_send, 'seq', split_axis=1, concat_axis=1, tiled=True)  26 us
    reduce_sum x4, other arithmetic, backward_step(): delta = jnp.sum(prob * dprob, axis=-1)  22.6 us
    unnamed x74, local copies, waits for them, and re-layouts  22.6 us
  transfers between devices with their start and end apart: 12, of which 6 were waited for; matrix products, arithmetic and copies ran while one was open for 7% of the time, Pallas kernels for 0%

profile of v1, /device:TPU:0, one launch (start us, length us, event | category | flops | bytes accessed | tf_op | source)
XLA Modules:
  0.0 686.1 jit_solution(5127588383337940336)
XLA Ops:
  21.4 6.0 collective-permute-start
  50.5 33.6 %collective-permute-done.3 = bf16[2,1,256,256]{3,2,1,0:T(8,128)(2,1)} collective-permute-done((bf16[2,1,256,256]{3,2,1,0:T(8,128)(2,1)}, bf16[2,1,256,256]{3,2,1,0:T(8,128)(2,1)}, u32[]{:S(2)}, u32[]{:S(2)}) %collective-permute-start.3) | collective-permute-done | bytes 262176 | tf_op jit(solution)/shard_map/ppermute | solution.py:23
  93.0 47.7 %all-reduce.5.cloned.1.call-done = bf16[2,4,256,256]{3,2,1,0:T(8,128)(2,1)} async-done(((bf16[2,4,256,256]{3,2,1,0:T(8,128)(2,1)}), bf16[2,4,256,256]{3,2,1,0:T(8,128)(2,1)}) %all-reduce.5.cloned.1.call-update) | async-done | bytes 1048592 | tf_op jit(solution)/shard_map/psum | solution.py:324
  141.9 76.7 %while.32 = (s32[]{:T(128)}, bf16[4,2,2,256,128]{4,3,2,0,1:T(8,128)(2,1)}, bf16[4,2,2,256,128]{4,3,2,1,0:T(8,128)(2,1)S(1)}, bf16[4,2,2,256,256]{4,3,2,1,0:T(8,1...) while((s32[]{:T(128)}, ...), condition=%wide.region_9.11_spmd.clone, body=%wide.region_6.10_spmd.clone.sunk | while | flops 818284032 | bytes 55597728 | solution.py:116
  148.5 5.4 copy.408
  167.7 5.4 copy.408
  186.9 5.4 copy.408
  206.1 5.4 copy.408
  223.1 7.1 %psum.36 = f32[8,256]{1,0:T(8,128)S(1)} all-reduce(f32[8,256]{1,0:T(8,128)S(1)} %reduce_sum.131), channel_id=1, replica_groups=mesh['seq'=8,'head'=4] {'head'}, use_global_device_ids=true, to_apply=%region_11.13 | all-reduce | flops 2048 | bytes 16384 | tf_op jit(solution)/shard_map/psum | solution.py:334
  233.1 6.1 psum.37
  243.6 236.4 %while.33 = (s32[]{:T(128)}, f32[2,4,256,256]{2,3,1,0:T(8,128)}, bf16[4,2,2,256,128]{4,3,2,0,1:T(8,128)(2,1)}, f32[4,2,2,256,256]{3,4,2,1,0:T(8,128)}, f32[4,2,2...) while((s32[]{:T(128)}, f32[2,4,256,256]{2,3,1,0:T(8,128)}, ...), condition=%wide.region_18.20_spmd.clone, body=%wide.region_14.19_spmd.clone.sunk | while | flops 1934750720 | bytes 250435856 | solution.py:230
  249.4 5.4 copy.411
  264.2 5.4 copy.410
  269.6 5.7 multiply_reduce_fusion.3
  307.3 5.4 copy.411
  322.1 5.4 copy.410
  327.6 5.7 multiply_reduce_fusion.3
  366.8 5.4 copy.411
  381.6 5.4 copy.410
  387.0 5.7 multiply_reduce_fusion.3
  426.3 5.4 copy.411
  441.1 5.4 copy.410
  446.5 5.7 multiply_reduce_fusion.3
  482.6 9.9 %all_to_all.25 = f32[2,8,256]{2,0,1:T(2,128)S(1)} all-to-all(f32[2,8,256]{2,0,1:T(2,128)S(1)} %get-tuple-element.380), channel_id=1, replica_groups=mesh['seq'=8,'head'=4] {'seq'}, dimensions={1} | all-to-all | bytes 32768 | tf_op jit(solution)/shard_map/all_to_all | solution.py:351
  507.3 4.9 all-to-all-done.4
  512.2 26.0 %all_to_all.26 = bf16[2,8,256,128]{3,2,0,1:T(8,128)(2,1)} all-to-all(bf16[2,8,256,128]{3,2,0,1:T(8,128)(2,1)} %get-tuple-element.381), channel_id=1, replica_groups=mesh['seq'=8,'head'=4] {'seq'}, dimensions={1} | all-to-all | bytes 2097152 | tf_op jit(solution)/shard_map/all_to_all | solution.py:313
  543.9 4.7 copy.282
  553.0 27.8 %psum.39 = f32[256]{0:T(256)} all-reduce(f32[256]{0:T(256)S(1)} %bitcast.413), channel_id=1, replica_groups=mesh['seq'=8,'head'=4] {'seq'}, use_global_device_ids=true, to_apply=%region_23.25 | all-reduce | flops 256 | bytes 2048 | tf_op jit(solution)/shard_map/psum | solution.py:364
  590.0 4.8 fusion.123
  596.2 64.2 %all-reduce.7.cloned.1.call-done = f32[2,4,256,256]{3,1,2,0:T(4,128)} async-done(((f32[2,4,256,256]{3,1,2,0:T(4,128)}), f32[2,4,256,256]{3,1,2,0:T(4,128)}) %all-reduce.7.cloned.1.call-update) | async-done | bytes 2097168 | tf_op jit(solution)/shard_map/psum | solution.py:364
  660.3 5.3 fusion.132
  665.6 5.3 copy.301
  (512 shorter events, 329.1 us)
Async XLA Ops:
  7.2 133.6 %all-reduce.5.cloned.1.call-start = ((), (), s32[]{:S(2)}) async-start(), calls=%async_computation.5 | async-start | bytes 2097152 | tf_op jit(solution)/shard_map/psum | solution.py:324
  18.2 12.7 %copy-start.36 = (s32[2,64]{1,0:T(2,128)S(1)}, s32[2,64]{1,0:T(2,128)}, u32[]{:S(2)}) copy-start(s32[2,64]{1,0:T(2,128)} %param.17) | copy-start | bytes 1540
  21.4 19.0 %collective-permute-start = (bf16[2,1,256,256]{3,2,1,0:T(8,128)(2,1)}, bf16[2,1,256,256]{3,2,1,0:T(8,128)(2,1)}, u32[]{:S(2)}, u32[]{:S(2)}) collective-permute-start(bf16[2,1,256,256]{3,2,1,0:T(8,128)(2,1)} %get-tuple-element.373), channel_id=1, source_target_pairs={{0,28},{4,0},{8,4},{12,8},{16,12},{20,16},{24,20},{28,24},{1,29},{... | collective-permute-start | bytes 786440 | tf_op jit(solution)/shard_map/ppermute | solution.py:23
  27.4 15.8 %collective-permute-start.1 = (bf16[2,1,256,256]{3,2,1,0:T(8,128)(2,1)}, bf16[2,1,256,256]{3,2,1,0:T(8,128)(2,1)}, u32[]{:S(2)}, u32[]{:S(2)}) collective-permute-start(bf16[2,1,256,256]{3,2,1,0:T(8,128)(2,1)} %get-tuple-element.372), channel_id=1, source_target_pairs={{0,24},{4,28},{8,0},{12,4},{16,8},{20,12},{24,16},{28,20},{1,25},{... | collective-permute-start | bytes 786440 | tf_op jit(solution)/shard_map/ppermute | solution.py:23
  27.9 21.6 %collective-permute-start.2 = (bf16[2,1,256,256]{3,2,1,0:T(8,128)(2,1)}, bf16[2,1,256,256]{3,2,1,0:T(8,128)(2,1)}, u32[]{:S(2)}, u32[]{:S(2)}) collective-permute-start(bf16[2,1,256,256]{3,2,1,0:T(8,128)(2,1)} %get-tuple-element.371), channel_id=1, source_target_pairs={{0,20},{4,24},{8,28},{12,0},{16,4},{20,8},{24,12},{28,16},{1,21},{... | collective-permute-start | bytes 786440 | tf_op jit(solution)/shard_map/ppermute | solution.py:23
  27.9 56.2 %collective-permute-start.3 = (bf16[2,1,256,256]{3,2,1,0:T(8,128)(2,1)}, bf16[2,1,256,256]{3,2,1,0:T(8,128)(2,1)}, u32[]{:S(2)}, u32[]{:S(2)}) collective-permute-start(bf16[2,1,256,256]{3,2,1,0:T(8,128)(2,1)} %get-tuple-element.370), channel_id=1, source_target_pairs={{0,16},{4,20},{8,24},{12,28},{16,0},{20,4},{24,8},{28,12},{1,17},{... | collective-permute-start | bytes 786440 | tf_op jit(solution)/shard_map/ppermute | solution.py:23
  30.9 54.2 %collective-permute-start.4 = (bf16[2,1,256,256]{3,2,1,0:T(8,128)(2,1)}, bf16[2,1,256,256]{3,2,1,0:T(8,128)(2,1)}, u32[]{:S(2)}, u32[]{:S(2)}) collective-permute-start(bf16[2,1,256,256]{3,2,1,0:T(8,128)(2,1)} %get-tuple-element.369), channel_id=1, source_target_pairs={{0,12},{4,16},{8,20},{12,24},{16,28},{20,0},{24,4},{28,8},{1,13},{... | collective-permute-start | bytes 786440 | tf_op jit(solution)/shard_map/ppermute | solution.py:23
  40.4 45.6 %collective-permute-start.5 = (bf16[2,1,256,256]{3,2,1,0:T(8,128)(2,1)S(1)}, bf16[2,1,256,256]{3,2,1,0:T(8,128)(2,1)S(1)}, u32[]{:S(2)}, u32[]{:S(2)}) collective-permute-start(bf16[2,1,256,256]{3,2,1,0:T(8,128)(2,1)S(1)} %copy-done.35), channel_id=1, source_target_pairs={{0,8},{4,12},{8,16},{12,20},{16,24},{20,28},{24,0},{28,4},{1,9},{5... | collective-permute-start | bytes 786440 | tf_op jit(solution)/shard_map/ppermute | solution.py:23
  43.2 42.9 %collective-permute-start.6 = (bf16[2,1,256,256]{3,2,1,0:T(8,128)(2,1)S(1)}, bf16[2,1,256,256]{3,2,1,0:T(8,128)(2,1)S(1)}, u32[]{:S(2)}, u32[]{:S(2)}) collective-permute-start(bf16[2,1,256,256]{3,2,1,0:T(8,128)(2,1)S(1)} %get-tuple-element.367), channel_id=1, source_target_pairs={{0,4},{4,8},{8,12},{12,16},{16,20},{20,24},{24,28},{28,0},{1,5},{5... | collective-permute-start | bytes 786440 | tf_op jit(solution)/shard_map/ppermute | solution.py:23
  89.9 52.0 %copy-start.47 = (s32[2]{0:T(128)S(1)}, s32[2]{0:T(128)}, u32[]{:S(2)}) copy-start(s32[2]{0:T(128)} %param.18) | copy-start | bytes 28
  218.6 11.7 %copy-start.22 = (f32[8,256,2,128]{3,2,1,0:T(2,128)S(1)}, f32[8,256,2,128]{3,2,1,0:T(2,128)}, u32[]{:S(2)}) copy-start(f32[8,256,2,128]{3,2,1,0:T(2,128)} %reshape.418) | copy-start | bytes 6291460
  218.6 11.7 %copy-start.46 = (f32[256]{0:T(256)S(1)}, f32[256]{0:T(256)}, u32[]{:S(2)}) copy-start(f32[256]{0:T(256)} %param.19) | copy-start | bytes 3076
  243.6 236.5 %copy-start.32 = (s32[16]{0:T(128)S(1)}, s32[16]{0:T(128)}, u32[]{:S(2)}) copy-start(s32[16]{0:T(128)} %reshape.321) | copy-start | bytes 196
  243.6 238.3 %copy-start.44 = (pred[2,8]{0,1:T(8,128)(4,1)S(1)}, pred[2,8]{0,1:T(8,128)(4,1)}, u32[]{:S(2)}) copy-start(pred[2,8]{0,1:T(8,128)(4,1)} %copy.283) | copy-start | bytes 52
  243.6 5.7 copy-start.7
  269.6 6.2 copy-start.2
  269.6 6.4 copy-start.6
  327.6 6.2 copy-start.2
  327.6 6.4 copy-start.6
  387.0 6.2 copy-start.2
  387.0 6.4 copy-start.6
  446.5 6.2 copy-start.2
  446.5 6.4 copy-start.6
  480.0 17.8 %copy-start.21 = (bf16[4,2,2,256,128]{4,3,2,0,1:T(8,128)(2,1)S(1)}, bf16[4,2,2,256,128]{4,3,2,0,1:T(8,128)(2,1)}, u32[]{:S(2)}) copy-start(bf16[4,2,2,256,128]{4,3,2,0,1:T(8,128)(2,1)} %get-tuple-element.606) | copy-start | bytes 3145732
  492.5 9.8 %all-to-all-start.2 = ((f32[2,8,256]{2,0,1:T(2,128)}), f32[2,8,256]{2,0,1:T(2,128)S(1)}, u32[]{:S(2)}, u32[]{:S(2)}) async-start(f32[2,8,256]{2,0,1:T(2,128)} %get-tuple-element.379), calls=%async_computation.2 | async-start | bytes 32768 | tf_op jit(solution)/shard_map/all_to_all | solution.py:352
  502.4 9.8 %all-to-all-start.4 = ((f32[2,8,256]{2,0,1:T(2,128)}), f32[2,8,256]{2,0,1:T(2,128)S(1)}, u32[]{:S(2)}, u32[]{:S(2)}) async-start(f32[2,8,256]{2,0,1:T(2,128)} %get-tuple-element.378), calls=%async_computation.4 | async-start | bytes 32768 | tf_op jit(solution)/shard_map/all_to_all | solution.py:353
  507.3 34.5 %copy-start.19 = (f32[2,4,256,256]{2,3,1,0:T(8,128)S(1)}, f32[2,4,256,256]{2,3,1,0:T(8,128)}, u32[]{:S(2)}) copy-start(f32[2,4,256,256]{2,3,1,0:T(8,128)} %get-tuple-element.121) | copy-start | bytes 6291460
  538.2 46.1 %all-to-all-start.3 = ((bf16[2,8,256,128]{3,2,0,1:T(8,128)(2,1)}), bf16[2,8,256,128]{3,2,0,1:T(8,128)(2,1)S(1)}, u32[]{:S(2)}, u32[]{:S(2)}) async-start(bf16[2,8,256,128]{3,2,0,1:T(8,128)(2,1)} %get-tuple-element.382), calls=%async_computation.3 | async-start | bytes 2097152 | tf_op jit(solution)/shard_map/all_to_all | solution.py:346
  541.8 118.6 %all-reduce.7.cloned.1.call-start = ((), (), s32[]{:S(2)}) async-start(), calls=%async_computation.6 | async-start | bytes 4194304 | tf_op jit(solution)/shard_map/psum | solution.py:364
  549.6 32.9 %copy-start.28 = (bf16[2,8,256,128]{3,2,0,1:T(8,128)(2,1)S(1)}, bf16[2,8,256,128]{3,2,0,1:T(8,128)(2,1)}, u32[]{:S(2)}) copy-start(bf16[2,8,256,128]{3,2,0,1:T(8,128)(2,1)} %all_to_all.26) | copy-start | bytes 3145732
  594.8 65.6 %copy-start.37 = (s32[2,4]{1,0:T(2,128)S(1)}, s32[2,4]{1,0:T(2,128)}, u32[]{:S(2)}) copy-start(s32[2,4]{1,0:T(2,128)} %get-tuple-element.352) | copy-start | bytes 100
  594.8 65.6 %copy-start.43 = (pred[2,4]{1,0:T(4,128)(4,1)S(1)}, pred[2,4]{1,0:T(4,128)(4,1)}, u32[]{:S(2)}) copy-start(pred[2,4]{1,0:T(4,128)(4,1)} %copy-done.42) | copy-start | bytes 28
  (88 other events, 259.4 us)
Sparse Core Ops, SparseCore 0:
  33.4 107.2 all-reduce.4
  546.2 114.0 all-reduce.6
